TPU v7x, 256 devices: a whole 4x4x8 slice. The times are simulated.
256 devices in a mesh: row: 64 (over y, z, core), col: 4 (over x).
Axes of the slice: x: 4, y: 4, z: 8, core: 2. Of those that a mesh axis runs over, the one named last changes fastest.
Arguments:
- matrix: bfloat16 [8192, 65536], P('col', 'row'), may hold values from -6 to 6
- prev_lower: bfloat16 [8192, 512], P('col'), may hold values from -1.1953125 to 1.1953125
- prev_upper: bfloat16 [512, 65536], P(None, 'row'), may hold values from -1.1953125 to 1.1953125
- lower_inverse: bfloat16 [512, 512], P('row'), as said below
- upper_inverse: bfloat16 [512, 512], P('col'), as said below
Outputs:
- factored: bfloat16 [8192, 65536], P('col', 'row')
Inputs may be any that keep to these rules, and one draw needn't show every extreme that they name: lower_inverse is unit lower triangular. upper_inverse is upper triangular with a positive diagonal.
All inputs are finite; a program needn't handle non-finite values.
Results may differ from a plain program's by a relative error of at most 0.0058.
Values may be sent and summed in bfloat16 or wider, within the bound.
A program may use at most 64 MiB of HBM per device.

v0:
```python
import jax
import jax.numpy as jnp
from jax import lax
from jax.sharding import PartitionSpec as P


def from_root(value, axis, source):
    kept = jnp.where(lax.axis_index(axis) == source, value, 0).astype(value.dtype)
    return lax.psum(kept, axis)


def local(matrix, prev_lower, prev_upper, lower_inverse, upper_inverse):
    rows_loc, cols_loc = matrix.shape
    block_width = upper_inverse.shape[1]
    row_pos = lax.axis_index("row")
    col_pos = lax.axis_index("col")
    lower_full = lax.all_gather(lower_inverse, "row", axis=0, tiled=True)
    upper_full = lax.all_gather(upper_inverse, "col", axis=0, tiled=True)
    panel_cols = matrix[:, :block_width]
    solved = jnp.dot(panel_cols, upper_full, preferred_element_type=jnp.float32).astype(
        jnp.bfloat16
    )
    lower_panel = from_root(solved, "row", 0)
    band_mask = (lax.broadcasted_iota(jnp.int32, (1, cols_loc), 1) < block_width) & (row_pos == 0)
    product = jnp.dot(prev_lower, prev_upper, preferred_element_type=jnp.float32)
    updated = (matrix.astype(jnp.float32) - product).astype(jnp.bfloat16)
    refreshed = lax.optimization_barrier(jnp.where(band_mask, matrix, updated))
    top_rows = refreshed[:block_width]
    lower_rows = refreshed[block_width:]
    solved_row = jnp.dot(lower_full, top_rows, preferred_element_type=jnp.float32).astype(
        jnp.bfloat16
    )
    upper_row = from_root(solved_row, "col", 0)

    def finish(stored, initial, lower_part, is_top):
        update = jnp.dot(lower_part, upper_row, preferred_element_type=jnp.float32)
        trailing = (stored.astype(jnp.float32) - update).astype(jnp.bfloat16)
        if is_top:
            pivot_rows = col_pos == 0
            first_cols = jnp.where(
                row_pos == 0,
                jnp.where(pivot_rows, initial[:, :block_width], lower_part),
                jnp.where(pivot_rows, upper_row[:, :block_width], trailing[:, :block_width]),
            )
            other_cols = jnp.where(
                pivot_rows, upper_row[:, block_width:], trailing[:, block_width:]
            )
        else:
            first_cols = jnp.where(row_pos == 0, lower_part, trailing[:, :block_width])
            other_cols = trailing[:, block_width:]
        return jnp.concatenate([first_cols, other_cols], 1)

    top_result = finish(top_rows, matrix[:block_width], lower_panel[:block_width], True)
    lower_result = finish(lower_rows, matrix[block_width:], lower_panel[block_width:], False)
    return jnp.concatenate([top_result, lower_result], 0)


def solution(mesh):
    in_specs = (P("col", "row"), P("col", None), P(None, "row"), P("row", None), P("col", None))
    out_specs = P("col", "row")
    return jax.shard_map(local, mesh=mesh, in_specs=in_specs, out_specs=out_specs, check_vma=False)
```

profile of v0, /device:TPU:73, one launch (start us, length us, event | category | flops | bytes accessed | tf_op | source)
XLA Modules:
  0.0 336.9 jit_solution(4852769366281387451)
XLA Ops:
  6.5 0.0 copy-start
  6.5 0.0 all-reduce.5.cloned.1.call-start
  6.5 1.6 copy-done
  8.1 0.0 copy-start.4
  8.1 8.5 %fusion = bf16[2048,1024]{1,0:T(8,128)(2,1)} fusion(bf16[2048,1024]{1,0:T(8,128)(2,1)} %param.5, pred[1024]{0:T(1024)(128)(4,1)S(1)} %fusion.9, bf16[2048,512]{1,0:T(8,128)(2,1)S(1)} %copy-done, bf16[512,1024]{1,0:T(8,128)(2,1)} %param.7), kind=kOutput, calls=%fused_computation.1 | convolution fusion | flops 2155872256 | bytes 11535360 | tf_op jit(solution)/shard_map/dot_general | solution.py:25
  16.6 0.0 copy-start.3
  16.6 0.0 copy-done.4
  16.6 51.0 %all_gather.7 = bf16[512,512]{1,0:T(8,128)(2,1)S(1)} all-gather(bf16[8,512]{1,0:T(8,128)(2,1)S(1)} %copy-done.4), channel_id=1, replica_groups=mesh['row'=64,'col'=4] {'row'}, dimensions={0}, use_global_device_ids=true | all-gather | bytes 532480 | tf_op jit(solution)/shard_map/all_gather | solution.py:17
  67.6 3.0 fusion.5
  70.6 0.0 all-reduce.5.cloned.1.call-update
  70.6 0.0 all-reduce.3.cloned.1.call-start
  70.6 0.0 copy-done.3
  70.6 11.1 %all_gather.6 = bf16[512,512]{1,0:T(8,128)(2,1)S(1)} all-gather(bf16[128,512]{1,0:T(8,128)(2,1)S(1)} %copy-done.3), channel_id=1, replica_groups=mesh['row'=64,'col'=4] {'col'}, dimensions={0}, use_global_device_ids=true | all-gather | bytes 655360 | tf_op jit(solution)/shard_map/all_gather | solution.py:18
  81.8 4.2 %fusion.1 = bf16[2048,512]{1,0:T(8,128)(2,1)} fusion(bf16[512,512]{1,0:T(8,128)(2,1)S(1)} %all_gather.6, bf16[2048,1024]{1,0:T(8,128)(2,1)} %param.5, pred[]{:T(512)S(6)} %eq.4), kind=kOutput, calls=%fused_computation.5 | convolution fusion | flops 1075838976 | bytes 4718593 | tf_op jit(solution)/shard_map/dot_general | solution.py:20
  85.9 0.0 all-reduce.3.cloned.1.call-update
  85.9 33.5 %all-reduce.5.cloned.1.call-done = bf16[512,1024]{1,0:T(8,128)(2,1)} async-done(((bf16[512,1024]{1,0:T(8,128)(2,1)}), bf16[512,1024]{1,0:T(8,128)(2,1)}) %all-reduce.5.cloned.1.call-update) | async-done | bytes 1048592 | tf_op jit(solution)/shard_map/psum | solution.py:9
  119.4 0.0 copy-start.2
  119.4 193.1 %all-reduce.3.cloned.1.call-done = bf16[2048,512]{1,0:T(8,128)(2,1)} async-done(((bf16[2048,512]{1,0:T(8,128)(2,1)}), bf16[2048,512]{1,0:T(8,128)(2,1)}) %all-reduce.3.cloned.1.call-update) | async-done | bytes 2097168 | tf_op jit(solution)/shard_map/psum | solution.py:9
  312.6 0.0 copy-start.1
  312.6 2.6 subtract_convert_fusion.2
  315.1 0.0 copy-done.2
  315.2 0.0 copy-done.1
  315.2 3.7 %subtract_convert_fusion.1 = bf16[1536,1024]{1,0:T(8,128)(2,1)S(1)} fusion(bf16[512,1024]{1,0:T(8,128)(2,1)S(1)} %copy-done.2, bf16[2048,1024]{1,0:T(8,128)(2,1)} %fusion, bf16[2048,512]{1,0:T(8,128)(2,1)S(1)} %copy-done.1), kind=kOutput, calls=%fused_computation.2 | convolution fusion | flops 1615331328 | bytes 8912896 | tf_op jit(solution)/shard_map/dot_general | solution.py:36
  318.9 1.2 fusion.7
  320.1 0.3 slice_select_fusion
  320.3 9.7 %maximum_maximum_fusion = bf16[2048,1024]{1,0:T(8,128)(2,1)} fusion(bf16[1536,512]{1,0:T(8,128)(2,1)S(1)} %get-tuple-element.6, bf16[1536,512]{1,0:T(8,128)(2,1)S(1)} %get-tuple-element.5, bf16[512,512]{1,0:T(8,128)(2,1)S(1)} %get-tuple-element.8, bf16[512,512]{1,0:T(8,128)(2,1)S(1)} %get-tuple-element.7), kind=kLoop, calls=%fused_computation.3 | loop fusion | flops 16777216 | bytes 8388608 | tf_op jit(solution)/shard_map/concatenate | solution.py:55
  (1 shorter events, 0.0 us)
Async XLA Ops:
  6.5 1.6 copy-start
  6.5 112.9 %all-reduce.5.cloned.1.call-start = ((), (), s32[]{:S(2)}) async-start(), calls=%async_computation.1 | async-start | bytes 2097152 | tf_op jit(solution)/shard_map/psum | solution.py:9
  8.1 8.5 %copy-start.4 = (bf16[8,512]{1,0:T(8,128)(2,1)S(1)}, bf16[8,512]{1,0:T(8,128)(2,1)}, u32[]{:S(2)}) copy-start(bf16[8,512]{1,0:T(8,128)(2,1)} %param.8) | copy-start | bytes 24580
  16.6 54.0 %copy-start.3 = (bf16[128,512]{1,0:T(8,128)(2,1)S(1)}, bf16[128,512]{1,0:T(8,128)(2,1)}, u32[]{:S(2)}) copy-start(bf16[128,512]{1,0:T(8,128)(2,1)} %param.9) | copy-start | bytes 393220
  70.6 242.0 %all-reduce.3.cloned.1.call-start = ((), (), s32[]{:S(2)}) async-start(), calls=%async_computation | async-start | bytes 4194304 | tf_op jit(solution)/shard_map/psum | solution.py:9
  119.4 195.7 %copy-start.2 = (bf16[512,1024]{1,0:T(8,128)(2,1)S(1)}, bf16[512,1024]{1,0:T(8,128)(2,1)}, u32[]{:S(2)}) copy-start(bf16[512,1024]{1,0:T(8,128)(2,1)} %all-reduce.5.cloned.1.call-done) | copy-start | bytes 3145732
  312.6 2.6 copy-start.1
Sparse Core Ops, SparseCore 0:
  70.7 48.6 all-reduce.4
  123.3 189.2 all-reduce.2
where the time goes:
time: 341 us; the launch traced here: 337 us
  waiting for transfers between devices  227 us (67%)
  blocking collectives  62.1 us (18%)
  matrix products  21.8 us (6%)
  between operations  13.5 us (4%)
  other arithmetic  11.2 us (3%)
    psum x2, waiting for transfers between devices, from_root(): return lax.psum(kept, axis)  227 us
    all_gather x1, blocking collectives, local(): lower_full = lax.all_gather(lower_inverse, 'row', axis=0, tiled=True)  51 us
    all_gather x1, blocking collectives, local(): upper_full = lax.all_gather(upper_inverse, 'col', axis=0, tiled=True)  11.1 us
    concatenate x1, other arithmetic, local(): return jnp.concatenate([top_result, lower_result], 0)  9.71 us
    dot_general x1, matrix products, local(): jnp.dot(prev_lower, prev_upper, preferred_element_type=jnp.float32)  8.49 us
  transfers between devices with their start and end apart: 2, of which 2 were waited for; matrix products, arithmetic and copies ran while one was open for 1% of the time, Pallas kernels for 0%

commit v1 on v0

v1 whole, which is shorter than its diff:
```python
import functools

import jax
import jax.numpy as jnp
from jax import lax
from jax.experimental import pallas as pl
from jax.experimental.pallas import tpu as pltpu
from jax.sharding import PartitionSpec as P

MESH = pl.DeviceIdType.MESH
NY, NZ, NX = 4, 8, 4
NB = 512
CH = 64
HOP = 3
EARLY = 3
F32 = jnp.float32
BF16 = jnp.bfloat16


def dot(a, b):
    return jnp.dot(a, b, preferred_element_type=F32)


def device(y, z, k, x):
    row = (lax.rem(y + NY, NY) * NZ + lax.rem(z + NZ, NZ)) * 2 + k
    return (row, lax.rem(x + NX, NX))


def kernel(m_hbm, pl_hbm, pu_hbm, li_hbm, ui_hbm, o_hbm,
           m, prev_l, prev_u, linv, uinv, lp, r0, ur, out,
           in_sem, out_sem, bar_unused, xss, xrs, pss, prs, zss, zrs, yss, yrs, kss, krs, uss, urs):
    rows = m.shape[0]
    n_chunk = rows // CH
    r = lax.axis_index("row")
    c = lax.axis_index("col")
    y, z, k = r // 16, (r // 2) % NZ, r % 2
    top = c == 0
    first = r == 0
    lo = jnp.where(top, NB // CH, 0)

    own_l = linv.at[y, z, k]
    loads = [
        pltpu.make_async_copy(li_hbm, own_l, in_sem.at[0]),
        pltpu.make_async_copy(ui_hbm, uinv.at[c], in_sem.at[1]),
        pltpu.make_async_copy(pu_hbm, prev_u, in_sem.at[2]),
        pltpu.make_async_copy(pl_hbm, prev_l, in_sem.at[3]),
        pltpu.make_async_copy(m_hbm, m, in_sem.at[4]),
    ]
    for load in loads:
        load.start()

    barrier = pltpu.get_barrier_semaphore()
    partners = [device(y, z + d, k, c) for d in range(1, NZ)]
    partners += [device(y + d, z, k, c) for d in range(1, NY)]
    partners += [device(y, z, k, c + d) for d in range(1, NX)]
    partners += [device(y, z, 1 - k, c)]
    partners += [device(y + dy, z + dz, 1 - k, c) for dy, dz in ((1, 0), (3, 0), (0, 1), (0, 7))]
    for partner in partners:
        pl.semaphore_signal(barrier, inc=1, device_id=partner, device_id_type=MESH)
    pl.semaphore_wait(barrier, len(partners))

    def remote(src, dst, send, recv, to):
        return pltpu.make_async_remote_copy(src_ref=src, dst_ref=dst, send_sem=send, recv_sem=recv,
                                            device_id=to, device_id_type=MESH)

    loads[0].wait()
    loads[1].wait()
    z_sends = [remote(own_l, own_l, zss.at[d - 1], zrs.at[z], device(y, z + d, k, c)) for d in range(1, NZ)]
    for copy in z_sends:
        copy.start()
    u_sends = [remote(uinv.at[c], uinv.at[c], uss.at[d - 1], urs.at[c], device(y, z, k, c + d)) for d in range(1, NX)]

    @pl.when(first)
    def _():
        for copy in u_sends:
            copy.start()

    loads[2].wait()
    loads[3].wait()
    loads[4].wait()

    def x_chunk(h, n):
        part = r0.at[h, n // 4, pl.ds(pl.multiple_of((n % 4) * 128, 128), 128)]
        to = device(y, z, k, c + 1 if h == 0 else c + 3)
        return remote(part, part, xss.at[h, n], xrs.at[h, n], to)

    @pl.when(top)
    def _():
        for p in range(4):
            for h in range(2):
                cols = slice(h * 512 + p * 128, h * 512 + p * 128 + 128)
                product = dot(prev_l[:NB], prev_u[:, cols])
                r0[h, p] = (m[:NB, cols].astype(F32) - product).astype(BF16)
            for i in range(4):
                for h in range(2):
                    x_chunk(h, 4 * p + i).start()

    def ref_chunk(i):
        return lp.at[pl.ds(pl.multiple_of(i * CH, CH), CH)]

    def p_send(i, d, to):
        return remote(ref_chunk(i), ref_chunk(i), pss.at[d, i], prs.at[i], to)

    def root_sends(i, q):
        kk = i % 2
        sends = {0: [(0, device(1, 0, kk, c))], 1: [(1, device(3, 0, kk, c))],
                 2: [(2, device(0, 1, kk, c)), (3, device(0, 7, kk, c))]}[q]
        return sends + [(4, device(0, 0, 1, c))]

    @pl.when(first)
    def _():
        for d in range(1, NX):
            src = lax.rem(c + d, NX)
            remote(uinv.at[src], uinv.at[src], uss.at[0], urs.at[src], device(y, z, k, c)).wait_recv()
        full = uinv[...].reshape(NB, NB)
        for t in range(rows // 256):
            def block():
                lp[t * 256:(t + 1) * 256] = dot(m[t * 256:(t + 1) * 256, :NB], full).astype(BF16)
                for i in range(t * 256 // CH, (t + 1) * 256 // CH):
                    for d, to in root_sends(i, i % 3):
                        p_send(i, d, to).start()
            if t * 256 < NB:
                pl.when(jnp.logical_not(top))(block)
            else:
                block()

    az = jnp.minimum(z, NZ - z)
    grow_up = z <= 3
    grow_down = jnp.logical_or(z == 0, jnp.logical_or(z == 6, z == 7))
    yes = {0: [], 1: [], 2: []}
    depth = []
    for q in range(2):
        yq = y if q == 0 else lax.rem(NY - y, NY)
        depth.append(az + jnp.where(yq == 1, 1, jnp.where(yq == 3, 3, 2)))
        at1 = yq == 1
        up = (0, 1) if q == 0 else (1, 0)
        fwd = jnp.logical_or(at1, yq == 2)
        back = jnp.logical_and(at1, z != 0)
        conds = [None] * 4
        conds[up[0]] = fwd
        conds[up[1]] = back
        conds[2] = jnp.logical_and(at1, grow_up)
        conds[3] = jnp.logical_and(at1, grow_down)
        yes[q] = conds
    dy = jnp.minimum(y, NY - y)
    depth.append(jnp.where(z == 0, dy + 2, az + dy))
    at0 = jnp.logical_and(y == 0, z != 0)
    yes[2] = [at0, at0, jnp.logical_and(y == 0, grow_up),
              jnp.logical_or(jnp.logical_and(y == 0, grow_down), jnp.logical_and(y != 0, z == 1))]
    one = jnp.logical_and(y == 1, z != 0)
    three = jnp.logical_and(y == 3, z != 0)
    root_chip = jnp.logical_and(y == 0, z == 0)

    def tree_sends(q, n, i):
        conds = list(yes[q])
        if q == 2:
            turn = (n // 2) % 2
            conds[0] = jnp.logical_or(conds[0], jnp.logical_and(one, turn == 0))
            conds[1] = jnp.logical_or(conds[1], jnp.logical_and(three, turn == 1))
        targets = [device(y + 1, z, k, c), device(y + 3, z, k, c), device(y, z + 1, k, c), device(y, z + 7, k, c)]
        sends = [(conds[d], p_send(i, d, targets[d])) for d in range(4)]
        sends.append((i >= 0, p_send(i, 4, device(y, z, 1 - k, c))))
        return sends

    def relays(n, q):
        i = 3 * n + q
        ok = jnp.logical_and(jnp.logical_and(i >= lo, i < n_chunk), jnp.logical_and(i % 2 == k, jnp.logical_not(root_chip)))
        return i, ok

    y_sends = [remote(linv.at[y, :, k], linv.at[y, :, k], yss.at[d - 1], yrs.at[y], device(y + d, z, k, c))
               for d in range(1, NY)]
    k_send = remote(linv.at[:, :, k], linv.at[:, :, k], kss.at[0], krs.at[0], device(y, z, 1 - k, c))

    n_x = 16
    steps = max(n_x + 3 * HOP, EARLY + 7 * HOP + n_chunk // 3 + 2)

    @pl.loop(0, steps)
    def _(s):
        @pl.when(s == 5)
        def _():
            for d in range(1, NZ):
                src = lax.rem(z + d, NZ)
                remote(own_l, linv.at[y, src, k], zss.at[0], zrs.at[src], device(y, z + 1, k, c)).wait_recv()
            for copy in y_sends:
                copy.start()

        @pl.when(s == 11)
        def _():
            for d in range(1, NY):
                src = lax.rem(y + d, NY)
                remote(linv.at[src, :, k], linv.at[src, :, k], yss.at[0], yrs.at[src],
                       device(y + 1, z, k, c)).wait_recv()
            k_send.start()

        for h in range(2):
            hop = c if h == 0 else lax.rem(NX - c, NX)
            n = s - HOP * (hop - 1)
            live = jnp.logical_and(jnp.logical_not(top), jnp.logical_and(n >= 0, n < n_x))

            @pl.when(live)
            def _():
                x_chunk(h, n).wait_recv()

            @pl.when(jnp.logical_and(live, hop < 3))
            def _():
                x_chunk(h, n).start()

        for q in range(3):
            n = s - EARLY - HOP * (depth[q] - 1) + jnp.where(top, 2, 0)
            i, ok = relays(n, q)

            @pl.when(ok)
            def _():
                p_send(i, 0, device(y + 1, z, k, c)).wait_recv()
                for cond, copy in tree_sends(q, n, i):
                    pl.when(cond)(copy.start)

        @pl.when(s < rows // 256)
        def _():
            tile = pl.ds(pl.multiple_of(s * 256, 256), 256)
            out[tile] = (m[tile].astype(F32) - dot(prev_l[tile], prev_u[...])).astype(BF16)

    @pl.loop(0, n_chunk)
    def _(i):
        mine = jnp.logical_and(i % 2 == k, jnp.logical_not(root_chip))

        @pl.when(jnp.logical_and(jnp.logical_and(i >= lo, jnp.logical_not(mine)), jnp.logical_not(first)))
        def _():
            p_send(i, 4, device(y, z, 1 - k, c)).wait_recv()

    remote(linv.at[:, :, 1 - k], linv.at[:, :, 1 - k], kss.at[0], krs.at[0], device(y, z, 1 - k, c)).wait_recv()

    full_l = linv[...].reshape(NB, NB)
    for p in range(4):
        ur[p] = dot(full_l, jnp.concatenate([r0[0, p], r0[1, p]], axis=1)).astype(BF16)

    stores = [pltpu.make_async_copy(out.at[pl.ds(t * NB, NB)], o_hbm.at[pl.ds(t * NB, NB)], out_sem.at[t])
              for t in range(rows // NB)]
    for t in range(rows // NB):
        tile = slice(t * NB, (t + 1) * NB)

        def body():
            for p in range(4):
                update = dot(lp[tile], ur[p])
                for h in range(2):
                    cols = slice(h * 512 + p * 128, h * 512 + p * 128 + 128)
                    part = update[:, h * 128:(h + 1) * 128]
                    value = (out[tile, cols].astype(F32) - part).astype(BF16)
                    if h == 0:
                        value = jnp.where(first, lp[tile, cols], value)
                    out[tile, cols] = value

        if t == 0:
            @pl.when(top)
            def _():
                for p in range(4):
                    for h in range(2):
                        cols = slice(h * 512 + p * 128, h * 512 + p * 128 + 128)
                        value = ur[p, :, h * 128:(h + 1) * 128]
                        if h == 0:
                            value = jnp.where(first, m[tile, cols], value)
                        out[tile, cols] = value

            pl.when(jnp.logical_not(top))(body)
        else:
            body()
        stores[t].start()

    for copy in z_sends + y_sends + [k_send]:
        copy.wait_send()

    @pl.when(first)
    def _():
        for copy in u_sends:
            copy.wait_send()
        for i in range(n_chunk):
            def done():
                for d, to in root_sends(i, i % 3):
                    p_send(i, d, to).wait_send()
            if i < NB // CH:
                pl.when(jnp.logical_not(top))(done)
            else:
                done()

    @pl.loop(0, n_x)
    def _(n):
        @pl.when(c <= 2)
        def _():
            x_chunk(0, n).wait_send()

        @pl.when(c != 1)
        def _():
            x_chunk(1, n).wait_send()

    @pl.loop(0, (n_chunk + 2) // 3)
    def _(n):
        for q in range(3):
            i, ok = relays(n, q)

            @pl.when(ok)
            def _():
                for cond, copy in tree_sends(q, n, i):
                    pl.when(cond)(copy.wait_send)

    for store in stores:
        store.wait()


def local(matrix, prev_lower, prev_upper, lower_inverse, upper_inverse):
    rows, cols = matrix.shape
    n_chunk = rows // CH
    dma = pltpu.SemaphoreType.DMA
    hbm = pl.BlockSpec(memory_space=pl.ANY)
    return pl.pallas_call(
        kernel,
        name="lu_step",
        out_shape=jax.ShapeDtypeStruct((rows, cols), BF16),
        in_specs=[hbm] * 5,
        out_specs=hbm,
        scratch_shapes=[
            pltpu.VMEM((rows, cols), BF16),
            pltpu.VMEM((rows, NB), BF16),
            pltpu.VMEM((NB, cols), BF16),
            pltpu.VMEM((NY, NZ, 2, 8, NB), BF16),
            pltpu.VMEM((NX, NB // NX, NB), BF16),
            pltpu.VMEM((rows, NB), BF16),
            pltpu.VMEM((2, 4, NB, 128), BF16),
            pltpu.VMEM((4, NB, 256), BF16),
            pltpu.VMEM((rows, cols), BF16),
            dma((5,)),
            dma((rows // NB,)),
            dma((1,)),
            dma((2, 16)),
            dma((2, 16)),
            dma((5, n_chunk)),
            dma((n_chunk,)),
            dma((NZ - 1,)),
            dma((NZ,)),
            dma((NY - 1,)),
            dma((NY,)),
            dma((1,)),
            dma((1,)),
            dma((NX - 1,)),
            dma((NX,)),
        ],
        compiler_params=pltpu.CompilerParams(collective_id=0, has_side_effects=True, vmem_limit_bytes=48 << 20),
        cost_estimate=pl.CostEstimate(flops=6 << 30, bytes_accessed=12 << 20, transcendentals=0),
    )(matrix, prev_lower, prev_upper, lower_inverse, upper_inverse)


def solution(mesh):
    in_specs = (P("col", "row"), P("col", None), P(None, "row"), P("row", None), P("col", None))
    out_specs = P("col", "row")
    return jax.shard_map(local, mesh=mesh, in_specs=in_specs, out_specs=out_specs, check_vma=False)
```

time: 341 us -> 64.4 us (0.19)
  the two profiles are of different devices: /device:TPU:73 before, /device:TPU:157 now
where the time goes in v1:
time: 64.4 us; the launch traced here: 64.1 us
  Pallas kernels  55.1 us (86%)
  local copies, waits for them, and re-layouts  9.06 us (14%)
    pallas_call x1, Pallas kernels, local(): pl.pallas_call(kernel, name='lu_step', out_shape=jax.ShapeDtypeStruct((ro...  55.1 us
    unnamed x9, local copies, waits for them, and re-layouts  9.06 us

profile of v1, /device:TPU:157, one launch (start us, length us, event | category | flops | bytes accessed | tf_op | source)
XLA Modules:
  0.0 64.1 jit_solution(3377680802349599176)
XLA Ops:
  0.0 0.0 copy-start
  0.0 1.6 %copy-done = bf16[2048,512]{1,0:T(8,128)(2,1)S(1)} copy-done((bf16[2048,512]{1,0:T(8,128)(2,1)S(1)}, bf16[2048,512]{1,0:T(8,128)(2,1)}, u32[]{:S(2)}) %copy-start) | copy-done | bytes 2097176
  1.6 0.0 copy-start.1
  1.6 1.2 %copy-done.1 = bf16[512,1024]{1,0:T(8,128)(2,1)S(1)} copy-done((bf16[512,1024]{1,0:T(8,128)(2,1)S(1)}, bf16[512,1024]{1,0:T(8,128)(2,1)}, u32[]{:S(2)}) %copy-start.1) | copy-done | bytes 1048600
  2.8 0.0 copy-start.2
  2.8 0.9 %copy-done.2 = bf16[128,512]{1,0:T(8,128)(2,1)S(1)} copy-done((bf16[128,512]{1,0:T(8,128)(2,1)S(1)}, bf16[128,512]{1,0:T(8,128)(2,1)}, u32[]{:S(2)}) %copy-start.2) | copy-done | bytes 131096
  3.7 0.0 copy-start.3
  3.7 0.7 %copy-done.3 = bf16[8,512]{1,0:T(8,128)(2,1)S(1)} copy-done((bf16[8,512]{1,0:T(8,128)(2,1)S(1)}, bf16[8,512]{1,0:T(8,128)(2,1)}, u32[]{:S(2)}) %copy-start.3) | copy-done | bytes 8216
  4.4 55.1 %lu_step.1 = bf16[2048,1024]{1,0:T(8,128)(2,1)} custom-call(bf16[2048,1024]{1,0:T(8,128)(2,1)} %m_hbm.1, bf16[2048,512]{1,0:T(8,128)(2,1)S(1)} %copy-done, bf16[512,1024]{1,0:T(8,128)(2,1)S(1)} %copy-done.1, bf16[8,512]{1,0:T(8,128)(2,1)S(1)} %copy-done.3, bf16[128,512]{1,0:T(8,128)(2,1)S(1)} %copy-done.2), custom_call_target="tpu_custom_call" | custom-call | flops 6442450944 | bytes 12582912 | tf_op jit(solution)/shard_map/lu_step/pallas_call | solution.py:314
  59.5 4.6 %copy.7 = bf16[2048,1024]{1,0:T(8,128)(2,1)} copy(bf16[2048,1024]{1,0:T(8,128)(2,1)} %lu_step.1) | data formatting | bytes 8388608
Async XLA Ops:
  0.0 1.6 %copy-start = (bf16[2048,512]{1,0:T(8,128)(2,1)S(1)}, bf16[2048,512]{1,0:T(8,128)(2,1)}, u32[]{:S(2)}) copy-start(bf16[2048,512]{1,0:T(8,128)(2,1)} %pl_hbm.1) | copy-start | bytes 6291460
  1.6 1.2 %copy-start.1 = (bf16[512,1024]{1,0:T(8,128)(2,1)S(1)}, bf16[512,1024]{1,0:T(8,128)(2,1)}, u32[]{:S(2)}) copy-start(bf16[512,1024]{1,0:T(8,128)(2,1)} %pu_hbm.1) | copy-start | bytes 3145732
  2.8 0.9 %copy-start.2 = (bf16[128,512]{1,0:T(8,128)(2,1)S(1)}, bf16[128,512]{1,0:T(8,128)(2,1)}, u32[]{:S(2)}) copy-start(bf16[128,512]{1,0:T(8,128)(2,1)} %ui_hbm.1) | copy-start | bytes 393220
  3.7 0.7 %copy-start.3 = (bf16[8,512]{1,0:T(8,128)(2,1)S(1)}, bf16[8,512]{1,0:T(8,128)(2,1)}, u32[]{:S(2)}) copy-start(bf16[8,512]{1,0:T(8,128)(2,1)} %li_hbm.1) | copy-start | bytes 24580

commit v2 on v0

v2 whole, which is shorter than its diff:
```python
import jax
import jax.numpy as jnp
from jax import lax
from jax.experimental import pallas as pl
from jax.experimental.pallas import tpu as pltpu
from jax.sharding import PartitionSpec as P

MESH = pl.DeviceIdType.MESH
NB = 512
CH = 64
HOP = 4
EARLY = 4
LATE = 4
SOLVE = 4
X_AT = 1
COUNT = (5, 5, 6)
N_X = 16
F32 = jnp.float32
BF16 = jnp.bfloat16


def dot(a, b):
    return jnp.dot(a, b, preferred_element_type=F32)


def both(a, b):
    return jnp.logical_and(a, b)


def either(a, b):
    return jnp.logical_or(a, b)


def remote(src, send, recv, to):
    return pltpu.make_async_remote_copy(src_ref=src, dst_ref=src, send_sem=send, recv_sem=recv,
                                        device_id=to, device_id_type=MESH)


def spread(m_hbm, pl_hbm, pu_hbm, li_hbm, ui_hbm, ref, lp, ur,
           m, prev_l, prev_u, linv, uinv, r0,
           in_sem, xss, xrs, pss, prs, prs2, prs3, zss, zrs, yss, yrs, kss, krs, uss, urs):
    rows = m.shape[0]
    r = lax.axis_index("row")
    c = lax.axis_index("col")
    y, z, k = r // 16, (r // 2) % 8, r % 2
    top = c == 0
    root = r == 0
    root_chip = r < 2

    own_l = linv.at[y, z, k]
    loads = [pltpu.make_async_copy(src, dst, in_sem.at[i]) for i, (src, dst) in enumerate((
        (li_hbm, own_l),
        (ui_hbm, uinv.at[c]),
        (pu_hbm, prev_u),
        (pl_hbm.at[pl.ds(0, NB)], prev_l.at[pl.ds(0, NB)]),
        (m_hbm.at[pl.ds(0, NB)], m.at[pl.ds(0, NB)]),
        (m_hbm.at[pl.ds(NB, rows - NB)], m.at[pl.ds(NB, rows - NB)]),
        (pl_hbm.at[pl.ds(NB, rows - NB)], prev_l.at[pl.ds(NB, rows - NB)]),
    ))]
    for load in loads:
        load.start()

    zs = [r + 2 * d - 16 * ((z + d) // 8) for d in range(1, 8)]
    ys = [r + 16 * d - 64 * ((y + d) // 4) for d in range(1, 4)]
    xs = [(c + d) % 4 for d in range(1, 4)]
    sib = (r + 1 - 2 * k, c)
    zp, zp2, zm2, zm = (zs[0], c), (zs[1], c), (zs[5], c), (zs[6], c)
    yp, ym = (ys[0], c), (ys[2], c)
    xp, xm = (r, xs[0]), (r, xs[2])

    def other(at):
        return (at[0] + 1 - 2 * k, c)

    barrier = pltpu.get_barrier_semaphore()

    def greet(at):
        pl.semaphore_signal(barrier, inc=1, device_id=at, device_id_type=MESH)

    for at in [zp, zm, yp, ym, sib] + [(r, a) for a in xs]:
        if at is zp:
            pl.when(zs[0] != 0)(lambda: greet(zp))
        else:
            greet(at)
    for at in (zp2, zm2):
        pl.when(at[0] != 0)(lambda at=at: greet(at))
    at_root = (0, c)
    for a in (3, 17, 49):
        pl.when(r == a)(lambda: greet(at_root))
    pl.when(r == 14)(lambda: greet((1, c)))
    pl.semaphore_wait(barrier, jnp.where(r == 1, 11, 10))

    loads[0].wait()
    loads[1].wait()

    def z_block(up, t):
        part = linv.at[y, (z - t) % 8 if up else (z + t) % 8, k]
        return remote(part, zss.at[0], zrs.at[0 if up else 1, t], zp if up else zm)

    def z_arrived(up, t):
        return remote(own_l, zss.at[0], zrs.at[0 if up else 1, t - 1], zp)

    def y_slab(up, t):
        part = linv.at[(y - t) % 4, :, k]
        return remote(part, yss.at[0], yrs.at[t if up else 2], yp if up else ym)

    def y_arrived(i):
        return remote(lp.at[pl.ds(0, 64)], yss.at[0], yrs.at[i], yp)

    z_block(True, 0).start()
    pl.when(r != 0)(z_block(False, 0).start)
    u_sends = [remote(uinv.at[c], uss.at[0], urs.at[0], (r, a)) for a in xs]

    @pl.when(root)
    def _():
        for copy in u_sends:
            copy.start()

    def x_chunk(h, n):
        part = r0.at[h, n // 4, pl.ds(pl.multiple_of((n % 4) * 128, 128), 128)]
        return remote(part, xss.at[h], xrs.at[h, n], xp if h == 0 else xm)

    for load in loads[2:5]:
        load.wait()

    @pl.when(top)
    def _():
        for p in range(4):
            cols = [slice(h * 512 + p * 128, h * 512 + p * 128 + 128) for h in range(2)]
            product = dot(prev_l[:NB], jnp.concatenate([prev_u[:, a] for a in cols], axis=1))
            for h in range(2):
                part = product[:, h * 128:(h + 1) * 128]
                r0[h, p] = (m[:NB, cols[h]].astype(F32) - part).astype(BF16)
            for i in range(4):
                for h in range(2):
                    x_chunk(h, 4 * p + i).start()

    for load in loads[5:]:
        load.wait()

    def p_chunk(j, kk):
        return lp.at[pl.ds(pl.multiple_of((2 * j + kk) * CH, CH), CH)]

    def p_send(j, kk, q, slot, to):
        return remote(p_chunk(j, kk), pss.at[q, slot], prs.at[j], to)

    def sib_send(j, kk):
        return remote(p_chunk(j, kk), pss.at[3, 0], prs2.at[0], sib)

    def sib_z_send(n, j, kk):
        return remote(p_chunk(j, kk), pss.at[3, 1], prs3.at[n, kk], sib)

    def place(n):
        return jnp.minimum(3 * n + 2, 15)

    def rows_of(n):
        return lp.at[pl.ds(0, n * CH)]

    def core(kk, at):
        return at if kk == 0 else other(at)

    @pl.when(root)
    def _():
        remote(lp.at[pl.ds(0, 384)], uss.at[0], urs.at[0], xp).wait_recv()
        full = uinv[...].reshape(NB, NB)
        for t in range(rows // 256):
            lp[t * 256:(t + 1) * 256] = dot(m[t * 256:(t + 1) * 256, :NB], full).astype(BF16)
            for j in (2 * t, 2 * t + 1):
                q = 2 if j == 15 else j % 3
                for kk in range(2):
                    p_send(j, kk, q, 0, core(kk, (yp, ym, zp)[q])).start()
                    if q == 2:
                        sib_z_send(5 if j == 15 else j // 3, j, kk).start()
                    else:
                        sib_send(j, kk).start()

    zero = z == 0
    z35 = either(z == 3, z == 5)
    z_later = jnp.where(zero, 0, jnp.where(either(z == 1, z == 7), 3, jnp.where(z35, 7, 10)))
    start = []
    slots = []
    up = either(zero, either(z == 1, z35))
    up_to = (jnp.where(z == 1, zs[1], zs[0]), c)
    down = either(zero, either(z == 7, z == 3))
    down_to = (jnp.where(z == 7, zs[5], zs[6]), c)
    for q in range(2):
        near, far = (1, 3) if q == 0 else (3, 1)
        ahead, back = (yp, ym) if q == 0 else (ym, yp)
        at1 = y == near
        start.append(EARLY + z_later + jnp.where(at1, 0, jnp.where(y == far, 2 * HOP + LATE, jnp.where(y == 0, HOP + LATE, HOP))))
        slots.append([
            (either(at1, y == 2), ahead),
            (both(at1, z != 0), back),
            (both(at1, up), up_to),
            (both(at1, down), down_to),
        ])
    dy = jnp.minimum(y, 4 - y)
    on = both(y == 0, z != 0)
    start.append(EARLY - HOP + jnp.where(zero, 3 + (dy + 1) * HOP + LATE, z_later + dy * HOP + jnp.where(both(y == 2, z != 1), LATE, 0)))
    slots.append([
        (on, yp),
        (on, ym),
        (both(on, up), up_to),
        (either(both(on, down), both(y != 0, z == 1)), down_to),
        (both(either(y == 1, y == 3), z != 0), (jnp.where(y == 1, ys[0], ys[2]), c)),
    ])
    turn = jnp.where(y == 1, 0, 1)
    relay = r >= 2

    k_send = remote(linv.at[:, :, k], kss.at[0], krs.at[0], sib)

    steps = max(SOLVE * 7 + 6, EARLY + 10 + 2 * HOP + LATE + 10 + 1)

    @pl.loop(0, steps)
    def _(s):
        for t in range(1, 5):
            @pl.when(s == SOLVE * t + 1)
            def _(t=t):
                z_arrived(True, t).wait_recv()
                if t == 1:
                    pl.when(root)(z_block(False, 0).start)
                if t < 4:
                    z_block(True, t).start()
                    z_arrived(False, t).wait_recv()
                    if t < 3:
                        z_block(False, t).start()
                else:
                    y_slab(True, 0).start()
                    y_slab(False, 0).start()

        @pl.when(s == SOLVE * 5 + 1)
        def _():
            y_arrived(0).wait_recv()
            y_slab(True, 1).start()
            y_arrived(2).wait_recv()

        @pl.when(s == SOLVE * 6 + 1)
        def _():
            y_arrived(1).wait_recv()
            k_send.start()

        for h in range(2):
            n = s - X_AT - jnp.where(c == 2, HOP, 0)

            @pl.when(both(either(c == 2, c == (1 if h == 0 else 3)), both(n >= 0, n < N_X)))
            def _():
                copy = x_chunk(h, n)
                copy.wait_recv()
                copy.start()

        for q in range(3):
            ahead = s - start[q]
            n = ahead // 2

            @pl.when(both(both(relay, ahead >= 0), both(ahead % 2 == 0, n < COUNT[q])))
            def _():
                j = 3 * n + q if q < 2 else place(n)
                p_send(j, k, q, 0, yp).wait_recv()
                for slot, (cond, to) in enumerate(slots[q]):
                    if slot == 4:
                        cond = both(cond, n % 2 == turn)
                    pl.when(cond)(p_send(j, k, q, slot, to).start)
                sib_send(j, k).start()

        back = s - EARLY + 1

        @pl.when(both(both(r == 1, back >= 0), both(back % 2 == 0, back < 2 * COUNT[2])))
        def _():
            n = back // 2
            for kk in range(2):
                sib_z_send(n, place(n), kk).wait_recv()
                p_send(place(n), kk, 2, 0, other(zm) if kk == 0 else zm).start()

        @pl.when(s < rows // 256)
        def _():
            tile = pl.ds(pl.multiple_of(s * 256, 256), 256)
            ref[tile] = (m[tile].astype(F32) - dot(prev_l[tile], prev_u[...])).astype(BF16)

        @pl.when(s == SOLVE * 7 + 1)
        def _():
            remote(lp.at[pl.ds(0, 256)], kss.at[0], krs.at[0], sib).wait_recv()

        p = s - SOLVE * 7 - 2

        @pl.when(both(p >= 0, p < 4))
        def _():
            for h in range(2):
                @pl.when(c == (3 if h == 0 else 1))
                def _():
                    for i in range(4):
                        x_chunk(h, 4 * p + i).wait_recv()

            full_l = linv[...].reshape(NB, NB)
            ur[p] = dot(full_l, jnp.concatenate([r0[0, p], r0[1, p]], axis=1)).astype(BF16)

    @pl.when(relay)
    def _():
        remote(rows_of(16), pss.at[3, 0], prs2.at[0], sib).wait_recv()

    @pl.when(r == 1)
    def _():
        remote(rows_of(20), pss.at[3, 0], prs2.at[0], sib).wait_recv()
        remote(rows_of(12), pss.at[2, 0], prs.at[0], zm).wait_send()

    @pl.when(both(top, root))
    def _():
        ref[:NB, :NB] = m[:NB, :NB]

    remote(lp.at[pl.ds(0, 56)], zss.at[0], zrs.at[0], zp).wait_send()
    remote(lp.at[pl.ds(0, 192)], yss.at[0], yrs.at[0], yp).wait_send()
    k_send.wait_send()

    @pl.when(c <= 2)
    def _():
        remote(r0.at[0], xss.at[0], xrs.at[0, 0], xp).wait_send()

    @pl.when(c != 1)
    def _():
        remote(r0.at[1], xss.at[1], xrs.at[1, 0], xm).wait_send()

    @pl.when(root)
    def _():
        remote(lp.at[pl.ds(0, 384)], uss.at[0], urs.at[0], xp).wait_send()
        for q in range(3):
            remote(rows_of(2 * COUNT[q]), pss.at[q, 0], prs.at[0], yp).wait_send()
        remote(rows_of(20), pss.at[3, 0], prs2.at[0], sib).wait_send()
        remote(rows_of(12), pss.at[3, 1], prs2.at[0], sib).wait_send()

    @pl.when(relay)
    def _():
        for q in range(3):
            for slot, (cond, to) in enumerate(slots[q]):
                n = 3 if slot == 4 else COUNT[q]
                pl.when(cond)(remote(rows_of(n), pss.at[q, slot], prs.at[0], to).wait_send)
        remote(rows_of(16), pss.at[3, 0], prs2.at[0], sib).wait_send()


def finish(ref, lp, ur, out):
    t = pl.program_id(0)
    size = out.shape[0]
    root = lax.axis_index("row") == 0
    pivot = both(lax.axis_index("col") == 0, t < NB // size)
    tile = pl.ds(pl.multiple_of(t * size, size), size)

    def columns(p, h):
        return slice(h * 512 + p * 128, h * 512 + p * 128 + 128)

    @pl.when(pivot)
    def _():
        for p in range(4):
            for h in range(2):
                value = ur[p, tile, h * 128:(h + 1) * 128]
                if h == 0:
                    value = jnp.where(root, ref[tile, columns(p, h)], value)
                out[:, columns(p, h)] = value

    @pl.when(pivot == False)
    def _():
        left = lp[tile]
        for p in range(4):
            update = dot(left, ur[p])
            for h in range(2):
                part = update[:, h * 128:(h + 1) * 128]
                value = (ref[tile, columns(p, h)].astype(F32) - part).astype(BF16)
                if h == 0:
                    value = jnp.where(root, left[:, columns(p, 0)], value)
                out[:, columns(p, h)] = value


def local(*args):
    rows, cols = args[0].shape
    dma = pltpu.SemaphoreType.DMA
    hbm = pl.BlockSpec(memory_space=pl.ANY)
    vmem = pl.BlockSpec(memory_space=pltpu.VMEM)
    args = [pltpu.with_memory_space_constraint(a, pltpu.MemorySpace.HBM) for a in args]
    ref, lp, ur = pl.pallas_call(
        spread,
        name="spread",
        out_shape=(pltpu.VMEM((rows, cols), BF16), pltpu.VMEM((rows, NB), BF16), pltpu.VMEM((4, NB, 256), BF16)),
        in_specs=[hbm] * 5,
        out_specs=(vmem, vmem, vmem),
        scratch_shapes=[
            pltpu.VMEM((rows, cols), BF16),
            pltpu.VMEM((rows, NB), BF16),
            pltpu.VMEM((NB, cols), BF16),
            pltpu.VMEM((4, 8, 2, 8, NB), BF16),
            pltpu.VMEM((4, NB // 4, NB), BF16),
            pltpu.VMEM((2, 4, NB, 128), BF16),
            dma((7,)),
            dma((2,)),
            dma((2, N_X)),
            dma((4, 5)),
            dma((16,)),
            dma((1,)),
            dma((COUNT[2], 2)),
            dma((1,)), dma((2, 4)),
            dma((1,)), dma((3,)),
            dma((1,)), dma((1,)),
            dma((1,)), dma((1,)),
        ],
        compiler_params=pltpu.CompilerParams(collective_id=0, has_side_effects=True, vmem_limit_bytes=40 << 20),
        cost_estimate=pl.CostEstimate(flops=4 << 30, bytes_accessed=7 << 20, transcendentals=0),
    )(*args)
    size = 256
    return pl.pallas_call(
        finish,
        name="finish",
        grid=(rows // size,),
        out_shape=jax.ShapeDtypeStruct((rows, cols), BF16),
        in_specs=[vmem] * 3,
        out_specs=pl.BlockSpec((size, cols), lambda t: (t, 0)),
        compiler_params=pltpu.CompilerParams(vmem_limit_bytes=16 << 20),
        cost_estimate=pl.CostEstimate(flops=2 << 30, bytes_accessed=4 << 20, transcendentals=0),
    )(ref, lp, ur)


def solution(mesh):
    in_specs = (P("col", "row"), P("col", None), P(None, "row"), P("row", None), P("col", None))
    out_specs = P("col", "row")
    return jax.shard_map(local, mesh=mesh, in_specs=in_specs, out_specs=out_specs, check_vma=False)
```

time: 341 us -> 48.1 us (0.14); the launches traced: 337 us -> 48 us
  waiting for transfers between devices: 227 us -> 0 us
  blocking collectives: 62.1 us -> 0 us
  Pallas kernels: 0 us -> 48 us
  matrix products: 21.8 us -> 0 us
  between operations: 13.5 us -> 0.01 us
  other arithmetic: 11.2 us -> 0 us
    psum x2 -> x0, waiting for transfers between devices: 227 us -> none  [from_root(): return lax.psum(kept, axis)]
    all_gather x2 -> x0, blocking collectives: 62.1 us -> none  [the longest x1 51 us: local(): lower_full = lax.all_gather(lower_inverse, 'row', axis=0, tiled=True)]
    pallas_call x0 -> x2, Pallas kernels: none -> 48 us  [the longest x1 42.9 us: local(): pl.pallas_call(spread, name='spread', out_shape=(pltpu.VMEM((rows, cols),...]
    dot_general x5 -> x0, matrix products: 21.8 us -> none  [the longest x1 8.49 us: local(): jnp.dot(prev_lower, prev_upper, preferred_element_type=jnp.float32)]
    concatenate x1 -> x0, other arithmetic: 9.71 us -> none  [local(): return jnp.concatenate([top_result, lower_result], 0)]
  transfers between devices with their start and end apart: 2 -> 0, of which waited for: 2 -> 0; matrix products, arithmetic and copies ran while one was open for 1% -> 0% of each run, Pallas kernels for 0% -> 0%
where the time goes in v2:
time: 48.1 us; the launch traced here: 48 us
  Pallas kernels  48 us (100%)
    pallas_call x1, Pallas kernels, local(): pl.pallas_call(spread, name='spread', out_shape=(pltpu.VMEM((rows, cols),...  42.9 us
    pallas_call x1, Pallas kernels, local(): pl.pallas_call(finish, name='finish', grid=(rows // size,), out_shape=jax...  5.13 us

profile of v2, /device:TPU:73, one launch (start us, length us, event | category | flops | bytes accessed | tf_op | source)
XLA Modules:
  0.0 48.0 jit_solution(4135191683690650052)
XLA Ops:
  0.0 42.9 %spread.1 = (bf16[2048,1024]{1,0:T(8,128)(2,1)S(1)}, bf16[2048,512]{1,0:T(8,128)(2,1)S(1)}, bf16[4,512,256]{2,1,0:T(8,128)(2,1)S(1)}) custom-call(bf16[2048,1024]{1,0:T(8,128)(2,1)} %m_hbm.1, bf16[2048,512]{1,0:T(8,128)(2,1)} %pl_hbm.1, bf16[512,1024]{1,0:T(8,128)(2,1)} %pu_hbm.1, bf16[8,512]{1,0:T(8,128)(2,1)} %li_hbm.1, bf16[128,512]{1,0:T(8,128)(2,1)} %ui_hbm.1), custom_call_target="tpu_custom_call" | custom-call | flops 4294967296 | bytes 7340032 | tf_op jit(solution)/shard_map/spread/pallas_call | solution.py:375
  42.9 5.1 %finish.1 = bf16[2048,1024]{1,0:T(8,128)(2,1)} custom-call(bf16[2048,1024]{1,0:T(8,128)(2,1)S(1)} %get-tuple-element.8.ref, bf16[2048,512]{1,0:T(8,128)(2,1)S(1)} %get-tuple-element.9.lp, bf16[4,512,256]{2,1,0:T(8,128)(2,1)S(1)} %get-tuple-element.10.ur), custom_call_target="tpu_custom_call" | custom-call | flops 2147483648 | bytes 4194304 | tf_op jit(solution)/shard_map/finish/pallas_call | solution.py:404

commit v3 on v2

--- a/solution.py
+++ b/solution.py
@@ -9,10 +9,10 @@
 NB = 512
 CH = 64
 HOP = 4
-EARLY = 4
+EARLY = 2
 LATE = 4
 SOLVE = 4
-X_AT = 1
+X_AT = 3
 COUNT = (5, 5, 6)
 N_X = 16
 F32 = jnp.float32
@@ -81,13 +81,15 @@
             pl.when(zs[0] != 0)(lambda: greet(zp))
         else:
             greet(at)
-    for at in (zp2, zm2):
-        pl.when(at[0] != 0)(lambda at=at: greet(at))
+    pl.when(z == 3)(lambda: greet(zm2))
+    pl.when(z == 5)(lambda: greet(zp2))
     at_root = (0, c)
     for a in (3, 17, 49):
         pl.when(r == a)(lambda: greet(at_root))
     pl.when(r == 14)(lambda: greet((1, c)))
-    pl.semaphore_wait(barrier, jnp.where(r == 1, 11, 10))
+    count = 8 + jnp.where(either(z == 1, z == 7), 1, 0)
+    count = jnp.where(root, 10, jnp.where(r == 1, 9, count))
+    pl.semaphore_wait(barrier, count)
 
     loads[0].wait()
     loads[1].wait()
@@ -400,7 +402,7 @@
         compiler_params=pltpu.CompilerParams(collective_id=0, has_side_effects=True, vmem_limit_bytes=40 << 20),
         cost_estimate=pl.CostEstimate(flops=4 << 30, bytes_accessed=7 << 20, transcendentals=0),
     )(*args)
-    size = 256
+    size = 512
     return pl.pallas_call(
         finish,
         name="finish",

time: 48.1 us -> 46.3 us (0.963)
  Pallas kernels: 48 us -> 46.2 us
    pallas_call x1, Pallas kernels: 5.13 us -> 3.72 us  [local(): pl.pallas_call(finish, name='finish', grid=(rows // size,), out_shape=jax...]
where the time goes in v3:
time: 46.3 us
  Pallas kernels  46.2 us (100%)
    pallas_call x1, Pallas kernels, local(): pl.pallas_call(spread, name='spread', out_shape=(pltpu.VMEM((rows, cols),...  42.5 us
    pallas_call x1, Pallas kernels, local(): pl.pallas_call(finish, name='finish', grid=(rows // size,), out_shape=jax...  3.72 us

profile of v3, /device:TPU:73, one launch (start us, length us, event | category | flops | bytes accessed | tf_op | source)
XLA Modules:
  0.0 46.3 jit_solution(15129078736963290316)
XLA Ops:
  0.0 42.5 %spread.1 = (bf16[2048,1024]{1,0:T(8,128)(2,1)S(1)}, bf16[2048,512]{1,0:T(8,128)(2,1)S(1)}, bf16[4,512,256]{2,1,0:T(8,128)(2,1)S(1)}) custom-call(bf16[2048,1024]{1,0:T(8,128)(2,1)} %m_hbm.1, bf16[2048,512]{1,0:T(8,128)(2,1)} %pl_hbm.1, bf16[512,1024]{1,0:T(8,128)(2,1)} %pu_hbm.1, bf16[8,512]{1,0:T(8,128)(2,1)} %li_hbm.1, bf16[128,512]{1,0:T(8,128)(2,1)} %ui_hbm.1), custom_call_target="tpu_custom_call" | custom-call | flops 4294967296 | bytes 7340032 | tf_op jit(solution)/shard_map/spread/pallas_call | solution.py:377
  42.5 3.7 %finish.1 = bf16[2048,1024]{1,0:T(8,128)(2,1)} custom-call(bf16[2048,1024]{1,0:T(8,128)(2,1)S(1)} %get-tuple-element.8.ref, bf16[2048,512]{1,0:T(8,128)(2,1)S(1)} %get-tuple-element.9.lp, bf16[4,512,256]{2,1,0:T(8,128)(2,1)S(1)} %get-tuple-element.10.ur), custom_call_target="tpu_custom_call" | custom-call | flops 2147483648 | bytes 4194304 | tf_op jit(solution)/shard_map/finish/pallas_call | solution.py:406

commit v4 on v3

--- a/solution.py
+++ b/solution.py
@@ -7,13 +7,13 @@
 
 MESH = pl.DeviceIdType.MESH
 NB = 512
-CH = 64
+CH = 32
 HOP = 4
 EARLY = 2
-LATE = 4
+LATE = 2
 SOLVE = 4
 X_AT = 3
-COUNT = (5, 5, 6)
+COUNT = (10, 10, 12)
 N_X = 16
 F32 = jnp.float32
 BF16 = jnp.bfloat16
@@ -152,7 +152,7 @@
         return remote(p_chunk(j, kk), pss.at[3, 1], prs3.at[n, kk], sib)
 
     def place(n):
-        return jnp.minimum(3 * n + 2, 15)
+        return jnp.where(n < 10, 3 * n + 2, n + 20)
 
     def rows_of(n):
         return lp.at[pl.ds(0, n * CH)]
@@ -166,12 +166,12 @@
         full = uinv[...].reshape(NB, NB)
         for t in range(rows // 256):
             lp[t * 256:(t + 1) * 256] = dot(m[t * 256:(t + 1) * 256, :NB], full).astype(BF16)
-            for j in (2 * t, 2 * t + 1):
-                q = 2 if j == 15 else j % 3
+            for j in range(4 * t, 4 * t + 4):
+                q = 2 if j >= 30 else j % 3
                 for kk in range(2):
                     p_send(j, kk, q, 0, core(kk, (yp, ym, zp)[q])).start()
                     if q == 2:
-                        sib_z_send(5 if j == 15 else j // 3, j, kk).start()
+                        sib_z_send(j - 20 if j >= 30 else j // 3, j, kk).start()
                     else:
                         sib_send(j, kk).start()
 
@@ -210,7 +210,7 @@
 
     k_send = remote(linv.at[:, :, k], kss.at[0], krs.at[0], sib)
 
-    steps = max(SOLVE * 7 + 6, EARLY + 10 + 2 * HOP + LATE + 10 + 1)
+    steps = max(SOLVE * 7 + 6, EARLY + 10 + 2 * HOP + LATE + COUNT[2])
 
     @pl.loop(0, steps)
     def _(s):
@@ -251,9 +251,9 @@
 
         for q in range(3):
             ahead = s - start[q]
-            n = ahead // 2
-
-            @pl.when(both(both(relay, ahead >= 0), both(ahead % 2 == 0, n < COUNT[q])))
+            n = ahead
+
+            @pl.when(both(relay, both(n >= 0, n < COUNT[q])))
             def _():
                 j = 3 * n + q if q < 2 else place(n)
                 p_send(j, k, q, 0, yp).wait_recv()
@@ -265,9 +265,9 @@
 
         back = s - EARLY + 1
 
-        @pl.when(both(both(r == 1, back >= 0), both(back % 2 == 0, back < 2 * COUNT[2])))
-        def _():
-            n = back // 2
+        @pl.when(both(r == 1, both(back >= 0, back < COUNT[2])))
+        def _():
+            n = back
             for kk in range(2):
                 sib_z_send(n, place(n), kk).wait_recv()
                 p_send(place(n), kk, 2, 0, other(zm) if kk == 0 else zm).start()
@@ -296,12 +296,12 @@
 
     @pl.when(relay)
     def _():
-        remote(rows_of(16), pss.at[3, 0], prs2.at[0], sib).wait_recv()
+        remote(rows_of(32), pss.at[3, 0], prs2.at[0], sib).wait_recv()
 
     @pl.when(r == 1)
     def _():
-        remote(rows_of(20), pss.at[3, 0], prs2.at[0], sib).wait_recv()
-        remote(rows_of(12), pss.at[2, 0], prs.at[0], zm).wait_send()
+        remote(rows_of(40), pss.at[3, 0], prs2.at[0], sib).wait_recv()
+        remote(rows_of(24), pss.at[2, 0], prs.at[0], zm).wait_send()
 
     @pl.when(both(top, root))
     def _():
@@ -324,16 +324,16 @@
         remote(lp.at[pl.ds(0, 384)], uss.at[0], urs.at[0], xp).wait_send()
         for q in range(3):
             remote(rows_of(2 * COUNT[q]), pss.at[q, 0], prs.at[0], yp).wait_send()
-        remote(rows_of(20), pss.at[3, 0], prs2.at[0], sib).wait_send()
-        remote(rows_of(12), pss.at[3, 1], prs2.at[0], sib).wait_send()
+        remote(rows_of(40), pss.at[3, 0], prs2.at[0], sib).wait_send()
+        remote(rows_of(24), pss.at[3, 1], prs2.at[0], sib).wait_send()
 
     @pl.when(relay)
     def _():
         for q in range(3):
             for slot, (cond, to) in enumerate(slots[q]):
-                n = 3 if slot == 4 else COUNT[q]
+                n = COUNT[q] // 2 if slot == 4 else COUNT[q]
                 pl.when(cond)(remote(rows_of(n), pss.at[q, slot], prs.at[0], to).wait_send)
-        remote(rows_of(16), pss.at[3, 0], prs2.at[0], sib).wait_send()
+        remote(rows_of(32), pss.at[3, 0], prs2.at[0], sib).wait_send()
 
 
 def finish(ref, lp, ur, out):
@@ -391,7 +391,7 @@
             dma((2,)),
             dma((2, N_X)),
             dma((4, 5)),
-            dma((16,)),
+            dma((32,)),
             dma((1,)),
             dma((COUNT[2], 2)),
             dma((1,)), dma((2, 4)),

time: 46.3 us -> 45.1 us (0.974); the launches traced: 46.3 us -> 44.3 us
  Pallas kernels: 46.2 us -> 44.3 us
    pallas_call x1, Pallas kernels: 42.5 us -> 40.6 us  [local(): pl.pallas_call(spread, name='spread', out_shape=(pltpu.VMEM((rows, cols),...]
where the time goes in v4:
time: 45.1 us; the launch traced here: 44.3 us
  Pallas kernels  44.3 us (98%)
    pallas_call x1, Pallas kernels, local(): pl.pallas_call(spread, name='spread', out_shape=(pltpu.VMEM((rows, cols),...  40.6 us
    pallas_call x1, Pallas kernels, local(): pl.pallas_call(finish, name='finish', grid=(rows // size,), out_shape=jax...  3.72 us

profile of v4, /device:TPU:73, one launch (start us, length us, event | category | flops | bytes accessed | tf_op | source)
XLA Modules:
  0.0 44.3 jit_solution(8446817254284406447)
XLA Ops:
  0.0 40.6 %spread.1 = (bf16[2048,1024]{1,0:T(8,128)(2,1)S(1)}, bf16[2048,512]{1,0:T(8,128)(2,1)S(1)}, bf16[4,512,256]{2,1,0:T(8,128)(2,1)S(1)}) custom-call(bf16[2048,1024]{1,0:T(8,128)(2,1)} %m_hbm.1, bf16[2048,512]{1,0:T(8,128)(2,1)} %pl_hbm.1, bf16[512,1024]{1,0:T(8,128)(2,1)} %pu_hbm.1, bf16[8,512]{1,0:T(8,128)(2,1)} %li_hbm.1, bf16[128,512]{1,0:T(8,128)(2,1)} %ui_hbm.1), custom_call_target="tpu_custom_call" | custom-call | flops 4294967296 | bytes 7340032 | tf_op jit(solution)/shard_map/spread/pallas_call | solution.py:377
  40.6 3.7 %finish.1 = bf16[2048,1024]{1,0:T(8,128)(2,1)} custom-call(bf16[2048,1024]{1,0:T(8,128)(2,1)S(1)} %get-tuple-element.8.ref, bf16[2048,512]{1,0:T(8,128)(2,1)S(1)} %get-tuple-element.9.lp, bf16[4,512,256]{2,1,0:T(8,128)(2,1)S(1)} %get-tuple-element.10.ur), custom_call_target="tpu_custom_call" | custom-call | flops 2147483648 | bytes 4194304 | tf_op jit(solution)/shard_map/finish/pallas_call | solution.py:406

commit v5 on v4

--- a/solution.py
+++ b/solution.py
@@ -172,8 +172,10 @@
                     p_send(j, kk, q, 0, core(kk, (yp, ym, zp)[q])).start()
                     if q == 2:
                         sib_z_send(j - 20 if j >= 30 else j // 3, j, kk).start()
-                    else:
-                        sib_send(j, kk).start()
+        for j in range(30):
+            for kk in range(2):
+                if j % 3 != 2:
+                    sib_send(j, kk).start()
 
     zero = z == 0
     z35 = either(z == 3, z == 5)

time: 45.1 us -> 45.3 us (level)
  the two profiles are of different devices: /device:TPU:73 before, /device:TPU:9 now
where the time goes in v5:
time: 45.3 us
  Pallas kernels  45.2 us (100%)
    pallas_call x1, Pallas kernels, local(): pl.pallas_call(spread, name='spread', out_shape=(pltpu.VMEM((rows, cols),...  41.5 us
    pallas_call x1, Pallas kernels, local(): pl.pallas_call(finish, name='finish', grid=(rows // size,), out_shape=jax...  3.72 us

profile of v5, /device:TPU:9, one launch (start us, length us, event | category | flops | bytes accessed | tf_op | source)
XLA Modules:
  0.0 45.3 jit_solution(17201768548527450213)
XLA Ops:
  0.0 41.5 %spread.1 = (bf16[2048,1024]{1,0:T(8,128)(2,1)S(1)}, bf16[2048,512]{1,0:T(8,128)(2,1)S(1)}, bf16[4,512,256]{2,1,0:T(8,128)(2,1)S(1)}) custom-call(bf16[2048,1024]{1,0:T(8,128)(2,1)} %m_hbm.1, bf16[2048,512]{1,0:T(8,128)(2,1)} %pl_hbm.1, bf16[512,1024]{1,0:T(8,128)(2,1)} %pu_hbm.1, bf16[8,512]{1,0:T(8,128)(2,1)} %li_hbm.1, bf16[128,512]{1,0:T(8,128)(2,1)} %ui_hbm.1), custom_call_target="tpu_custom_call" | custom-call | flops 4294967296 | bytes 7340032 | tf_op jit(solution)/shard_map/spread/pallas_call | solution.py:379
  41.5 3.7 %finish.1 = bf16[2048,1024]{1,0:T(8,128)(2,1)} custom-call(bf16[2048,1024]{1,0:T(8,128)(2,1)S(1)} %get-tuple-element.8.ref, bf16[2048,512]{1,0:T(8,128)(2,1)S(1)} %get-tuple-element.9.lp, bf16[4,512,256]{2,1,0:T(8,128)(2,1)S(1)} %get-tuple-element.10.ur), custom_call_target="tpu_custom_call" | custom-call | flops 2147483648 | bytes 4194304 | tf_op jit(solution)/shard_map/finish/pallas_call | solution.py:408
